TPU v7x, 32 devices: a whole 2x2x4 slice. The times are simulated.
32 devices in a mesh: group: 2 (over y), ctx: 4 (over x, core), tp: 4 (over z).
Axes of the slice: x: 2, y: 2, z: 4, core: 2. Of those that a mesh axis runs over, the one named last changes fastest.
Arguments:
- tokens: bfloat16 [1024, 5376], P(('group', 'ctx'), 'tp'), parts along dimension 0
- positions: int32 [1024], P(('group', 'ctx')), parts along dimension 0, may hold values from 0 to 383, as said below
- first_key: int32 [1024], P(('group', 'ctx')), parts along dimension 0, may hold values from 0 to 511, as said below
- input_gain: float32 [5376], replicated, may hold values from 0.1 to 1.9
- query_weight: bfloat16 [5376, 4096], P(None, 'tp'), may hold values from -0.078125 to 0.078125
- kv_weight: bfloat16 [2, 5376, 2048], P(None, None, 'tp'), may hold values from -0.078125 to 0.078125
- query_gain: float32 [128], replicated, may hold values from 0.1 to 1.9
- key_gain: float32 [128], replicated, may hold values from 0.1 to 1.9
- out_weight: bfloat16 [4096, 5376], P('tp'), may hold values from -0.125 to 0.125
- post_gain: float32 [5376], replicated, may hold values from 0.1 to 1.9
Outputs:
- layer_out: bfloat16 [1024, 5376], P(('group', 'ctx'), 'tp'), parts along dimension 0
There are 2 independent parts, one for each index of `group`. A program takes and returns all parts, laid end to end along the dimension named above; an argument that names none is the same for every part. Nothing has to cross between parts.
Inputs may be any that keep to these rules, and one draw needn't show every extreme that they name: `positions`: A token's position is its offset within its document. Documents are contiguous runs of tokens; exactly one of them is 384 tokens long, every other one is shorter, and the last token forms a document of its own. first_key[i] is the larger of i - 1023 and the index of the first token of i's document (documents as described for positions).
All inputs are finite; a program needn't handle non-finite values.
Results may differ from a plain program's by a relative error of at most 0.014.
Values may be sent and summed in bfloat16 or wider, within the bound.
A program may use at most 128 MiB of HBM per device.

v0:
```python
import math
import jax
import jax.numpy as jnp
from jax import lax
from jax.sharding import PartitionSpec as P

D = 5376
H = 32
WINDOW = 1024
EPSILON = 1e-06


def from_partner(array, axis, distance):
    return lax.ppermute(array, axis, [(i, i ^ 1 << distance) for i in range(lax.axis_size(axis))])


def passed_along(block, axis, distance):
    devices = range(lax.axis_size(axis))
    route = [(i - distance, i) for i in devices if i - distance in devices]
    return lax.ppermute(block, axis, route)


def rms_norm(values, gain_vec):
    return (
        values * lax.rsqrt(jnp.mean(values * values, axis=-1, keepdims=True) + EPSILON) * gain_vec
    )


def rotate(values, positions_in):
    half_dim = values.shape[-1] // 2
    frequency = jnp.exp(
        jnp.arange(half_dim, dtype=jnp.float32) * (-2.0 * math.log(10000.0) / values.shape[-1])
    )
    angles = positions_in.astype(jnp.float32)[:, None] * frequency[None, :]
    cosines = jnp.cos(angles)[:, None, :]
    sine_part = jnp.sin(angles)[:, None, :]
    lower_half = values[..., :half_dim]
    upper_half = values[..., half_dim:]
    return jnp.concatenate(
        [
            lower_half * cosines - upper_half * sine_part,
            upper_half * cosines + lower_half * sine_part,
        ],
        axis=-1,
    )


def per_device(
    tokens,
    positions,
    first_key,
    input_gain,
    query_weight,
    kv_weight,
    query_gain,
    key_gain,
    out_weight,
    post_gain,
):
    tok_rows = tokens.shape[0]
    feat_dev = tokens.shape[1]
    head_dim = query_gain.shape[0]
    heads_dev = query_weight.shape[1] // head_dim
    tp_index = lax.axis_index("tp")
    ctx_index = lax.axis_index("ctx")
    ctx_count = lax.axis_size("ctx")
    local_x = tokens.astype(jnp.float32)
    kv_full = kv_weight
    if heads_dev == 1:
        partner = from_partner(kv_weight, "tp", 0)
        is_even = tp_index % 2 == 0
        kv_full = jnp.where(
            is_even,
            jnp.concatenate([kv_weight, partner], axis=2),
            jnp.concatenate([partner, kv_weight], axis=2),
        )
    gathered = lax.all_gather(tokens, "tp", axis=1, tiled=True).astype(jnp.float32)
    normed = rms_norm(gathered, input_gain).astype(jnp.bfloat16)
    query_raw = jnp.dot(normed, query_weight, preferred_element_type=jnp.float32)
    key_raw = jnp.dot(normed, kv_full[0], preferred_element_type=jnp.float32)
    value_raw = jnp.dot(normed, kv_full[1], preferred_element_type=jnp.float32)
    kv_heads = key_raw.shape[1] // head_dim
    group_size = heads_dev // kv_heads
    queries = (
        rotate(rms_norm(query_raw.reshape(tok_rows, heads_dev, head_dim), query_gain), positions)
        * (D // H) ** (-0.5)
    ).astype(jnp.bfloat16)
    keys = rotate(
        rms_norm(key_raw.reshape(tok_rows, kv_heads, head_dim), key_gain), positions
    ).astype(jnp.bfloat16)
    values_b = value_raw.reshape(tok_rows, kv_heads, head_dim).astype(jnp.bfloat16)
    kv_block = jnp.stack([keys, values_b])
    reach_blocks = min(ctx_count - 1, (WINDOW + tok_rows - 2) // tok_rows)
    received = []
    moving = kv_block
    for offset in range(reach_blocks):
        moving = passed_along(moving, "ctx", 1)
        received.append(moving)
    blocks = received[::-1] + [kv_block]
    keys_all = jnp.concatenate(blocks, axis=1)
    key_count = keys_all.shape[1]
    key_index = (ctx_index - reach_blocks) * tok_rows + jnp.arange(key_count, dtype=jnp.int32)
    query_index = ctx_index * tok_rows + jnp.arange(tok_rows, dtype=jnp.int32)
    visible = (key_index[None, :] >= first_key[:, None]) & (
        key_index[None, :] <= query_index[:, None]
    )
    grouped = queries.reshape(tok_rows, kv_heads, group_size, head_dim)
    scores = jnp.einsum("qkgd,tkd->kgqt", grouped, keys_all[0], preferred_element_type=jnp.float32)
    scores = jnp.where(visible[None, None], scores, -1e30)
    row_max = jnp.max(scores, axis=-1, keepdims=True)
    weights = jnp.exp(scores - row_max)
    denominator = jnp.sum(weights, axis=-1)
    mixed_out = jnp.einsum(
        "kgqt,tkd->qkgd",
        weights.astype(jnp.bfloat16),
        keys_all[1],
        preferred_element_type=jnp.float32,
    )
    mixed_out = mixed_out / jnp.transpose(denominator, (2, 0, 1))[..., None]
    attn = mixed_out.astype(jnp.bfloat16).reshape(tok_rows, heads_dev * head_dim)
    partial_value = jnp.dot(attn, out_weight, preferred_element_type=jnp.float32)
    summed = lax.psum(partial_value.astype(jnp.bfloat16), "tp").astype(jnp.float32)
    post_normed = rms_norm(summed, post_gain)
    own_cols = lax.dynamic_slice_in_dim(post_normed, tp_index * feat_dev, feat_dev, 1)
    return (local_x + own_cols).astype(jnp.bfloat16)


def solution(mesh):
    return jax.shard_map(
        per_device,
        mesh=mesh,
        in_specs=(
            P(("group", "ctx"), "tp"),
            P(("group", "ctx")),
            P(("group", "ctx")),
            P(),
            P(None, "tp"),
            P(None, None, "tp"),
            P(),
            P(),
            P("tp", None),
            P(),
        ),
        out_specs=P(("group", "ctx"), "tp"),
        check_vma=False,
    )
```

profile of v0, /device:TPU:0, one launch (start us, length us, event | category | flops | bytes accessed | tf_op | source)
XLA Modules:
  0.0 162.3 jit_solution(8768444792018409563)
XLA Ops:
  6.5 0.7 all-gather.2.cloned.1.call-update
  7.3 8.9 %slice_bitcast_fusion.1 = (bf16[512,5376]{0,1:T(8,128)(2,1)}, bf16[512,5376]{0,1:T(8,128)(2,1)}) fusion(bf16[2,5376,512]{2,1,0:T(8,128)(2,1)} %param.15), kind=kLoop, calls=%fused_computation.2 | loop fusion | bytes 22020096 | tf_op jit(solution)/shard_map/dot_general | solution.py:80
  16.3 8.3 %copy.37 = bf16[512,5376]{1,0:T(8,128)(2,1)} copy(bf16[512,5376]{0,1:T(8,128)(2,1)} %get-tuple-element.5) | data formatting | bytes 11010048 | tf_op jit(solution)/shard_map/dot_general | solution.py:80
  24.6 8.3 %copy.39 = bf16[512,5376]{1,0:T(8,128)(2,1)} copy(bf16[512,5376]{0,1:T(8,128)(2,1)} %get-tuple-element.6) | data formatting | bytes 11010048 | tf_op jit(solution)/shard_map/dot_general | solution.py:81
  32.9 0.2 multiply_cosine_fusion
  33.3 0.1 compare_and_fusion
  33.5 11.8 %all-gather.2.cloned.1.call-done = bf16[128,5376]{0,1:T(8,128)(2,1)} async-done(((bf16[128,1344]{0,1:T(8,128)(2,1)}), bf16[128,5376]{0,1:T(8,128)(2,1)}) %all-gather.2.cloned.1.call-update) | async-done | bytes 1376272 | tf_op jit(solution)/shard_map/all_gather | solution.py:77
  45.3 2.1 %fusion = f32[128]{0:T(128)S(1)} fusion(bf16[128,5376]{0,1:T(8,128)(2,1)} %all-gather.2.cloned.1.call-done), kind=kLoop, calls=%fused_computation.5 | loop fusion | flops 2064256 | bytes 1376768 | tf_op jit(solution)/shard_map/reduce_sum | solution.py:25
  47.4 4.8 %multiply_reduce_fusion.2 = (f32[128,4]{0,1:T(4,128)S(1)}, f32[128,4,128]{0,2,1:T(8,128)S(1)}) fusion(bf16[4,128,5376]{2,1,0:T(8,128)(2,1)} %bitcast.74, f32[5376]{0:T(1024)S(1)} %copy-done.4, f32[128]{0:T(128)S(1)} %add_rsqrt_fusion.3, bf16[128,5376]{0,1:T(8,128)(2,1)} %all-gather.2.cloned.1.call-done), kind=kOutput, calls=%fused_computation.44 | convolution fusion | flops 707526144 | bytes 7167488 | tf_op jit(solution)/shard_map/dot_general | solution.py:80
  52.4 1.7 %fusion.15 = bf16[1,128,4,128]{1,3,2,0:T(8,128)(2,1)S(1)} fusion(bf16[4,128,5376]{2,1,0:T(8,128)(2,1)S(1)} %bitcast.73, bf16[128,5376]{0,1:T(8,128)(2,1)S(1)} %copy-done, f32[5376]{0:T(1024)S(1)} %copy-done.4, f32[128]{0:T(128)S(1)} %add_rsqrt_fusion.3), kind=kOutput, calls=%fused_computation.23 | convolution fusion | flops 707461120 | bytes 7034368 | tf_op jit(solution)/shard_map/dot_general | solution.py:81
  54.2 1.3 collective-permute-start
  55.5 6.4 %convolution_bitcast_fusion.1 = f32[16,8,8,128]{3,1,2,0:T(8,128)S(1)} fusion(bf16[5376,1024]{1,0:T(8,128)(2,1)} %param.14, bf16[128,5376]{0,1:T(8,128)(2,1)S(1)} %copy-done, f32[5376]{0:T(1024)S(1)} %copy-done.4, f32[128]{0:T(128)S(1)} %add_rsqrt_fusion.3), kind=kOutput, calls=%fused_computation.20 | convolution fusion | flops 1412038656 | bytes 12932608 | tf_op jit(solution)/shard_map/dot_general | solution.py:79
  62.0 0.2 multiply_reduce_fusion.1
  62.3 4.1 %collective-permute-start.1 = (bf16[2,128,4,128]{1,3,2,0:T(8,128)(2,1)S(1)}, bf16[2,128,4,128]{1,3,2,0:T(8,128)(2,1)S(1)}, u32[]{:S(2)}, u32[]{:S(2)}) collective-permute-start(bf16[2,128,4,128]{1,3,2,0:T(8,128)(2,1)S(1)} %collective-permute-done), channel_id=1, source_target_pairs={{0,4},{4,8},{8,12},{1,5},{5,9},{9,13},{2,6},{6,10},{10,14},{3,7},{... | collective-permute-start | bytes 786440 | tf_op jit(solution)/shard_map/ppermute | solution.py:20
  66.6 0.2 multiply_multiply_fusion
  66.8 0.8 collective-permute-done.1
  67.6 4.3 %collective-permute-start.2 = (bf16[2,128,4,128]{1,3,2,0:T(8,128)(2,1)S(1)}, bf16[2,128,4,128]{1,3,2,0:T(8,128)(2,1)S(1)}, u32[]{:S(2)}, u32[]{:S(2)}) collective-permute-start(bf16[2,128,4,128]{1,3,2,0:T(8,128)(2,1)S(1)} %collective-permute-done.1), channel_id=1, source_target_pairs={{0,4},{4,8},{8,12},{1,5},{5,9},{9,13},{2,6},{6,10},{10,14},{3,7},{... | collective-permute-start | bytes 786440 | tf_op jit(solution)/shard_map/ppermute | solution.py:20
  71.8 0.3 multiply_subtract_fusion
  72.1 0.1 copy.46
  72.2 0.1 copy.47
  72.3 0.5 collective-permute-done.2
  72.8 0.1 maximum_maximum_fusion
  72.9 0.6 fusion.3
  73.6 0.4 fusion.4
  73.9 0.6 fusion.11
  74.5 9.6 %convolution_convert_fusion = bf16[128,5376]{0,1:T(8,128)(2,1)} fusion(bf16[128,1024]{0,1:T(8,128)(2,1)S(1)} %bitcast.78, bf16[1024,5376]{1,0:T(8,128)(2,1)} %param.18), kind=kOutput, calls=%fused_computation | convolution fusion | flops 1409974272 | bytes 12648448 | tf_op jit(solution)/shard_map/dot_general | solution.py:121
  84.2 0.8 dynamic-slice
  84.9 66.4 %all-reduce.2.cloned.1.call-done = bf16[128,5376]{0,1:T(8,128)(2,1)} async-done(((bf16[128,5376]{0,1:T(8,128)(2,1)}), bf16[128,5376]{0,1:T(8,128)(2,1)}) %all-reduce.2.cloned.1.call-update) | async-done | bytes 1376272 | tf_op jit(solution)/shard_map/psum | solution.py:122
  151.3 2.2 %multiply_reduce_fusion = f32[128]{0:T(128)S(1)} fusion(bf16[128,5376]{0,1:T(8,128)(2,1)} %all-reduce.2.cloned.1.call-done), kind=kLoop, calls=%fused_computation.8 | loop fusion | flops 2064256 | bytes 1376768 | tf_op jit(solution)/shard_map/reduce_sum | solution.py:25
  153.5 0.2 convert_element_type.52
  153.7 0.8 copy-done.3
  154.5 1.0 fusion.24
  (37 shorter events, 0.7 us)
Async XLA Ops:
  6.5 38.8 %all-gather.2.cloned.1.call-start = ((), (), s32[]{:S(2)}) async-start(), calls=%async_computation | async-start | bytes 1720320 | tf_op jit(solution)/shard_map/all_gather | solution.py:77
  7.3 144.1 %all-reduce.2.cloned.1.call-start = ((), (), s32[]{:S(2)}) async-start(), calls=%async_computation.1 | async-start | bytes 2752512 | tf_op jit(solution)/shard_map/psum | solution.py:122
  16.3 8.3 %copy-start.8 = (s32[128]{0:T(128)S(1)}, s32[128]{0:T(128)}, u32[]{:S(2)}) copy-start(s32[128]{0:T(128)} %param.11) | copy-start | bytes 1540
  24.6 8.7 %copy-start.5 = (s32[128]{0:T(128)S(1)}, s32[128]{0:T(128)}, u32[]{:S(2)}) copy-start(s32[128]{0:T(128)} %param.12) | copy-start | bytes 1540
  24.6 22.8 %copy-start.4 = (f32[5376]{0:T(1024)S(1)}, f32[5376]{0:T(1024)}, u32[]{:S(2)}) copy-start(f32[5376]{0:T(1024)} %param.13) | copy-start | bytes 64516
  47.4 4.9 %copy-start.6 = (f32[128]{0:T(128)S(1)}, f32[128]{0:T(128)}, u32[]{:S(2)}) copy-start(f32[128]{0:T(128)} %param.17) | copy-start | bytes 1540
  47.4 5.0 %copy-start = (bf16[128,5376]{0,1:T(8,128)(2,1)S(1)}, bf16[128,5376]{0,1:T(8,128)(2,1)}, u32[]{:S(2)}) copy-start(bf16[128,5376]{0,1:T(8,128)(2,1)} %all-gather.2.cloned.1.call-done) | copy-start | bytes 4128772
  47.4 5.0 %copy-start.1 = (bf16[512,5376]{1,0:T(8,128)(2,1)S(1)}, bf16[512,5376]{1,0:T(8,128)(2,1)}, u32[]{:S(2)}) copy-start(bf16[512,5376]{1,0:T(8,128)(2,1)} %copy.39) | copy-start | bytes 16515076
  54.2 12.4 %copy-start.7 = (f32[128]{0:T(128)S(1)}, f32[128]{0:T(128)}, u32[]{:S(2)}) copy-start(f32[128]{0:T(128)} %param.16) | copy-start | bytes 1540
  54.2 8.1 %collective-permute-start = (bf16[2,128,4,128]{1,3,2,0:T(8,128)(2,1)S(1)}, bf16[2,128,4,128]{1,3,2,0:T(8,128)(2,1)S(1)}, u32[]{:S(2)}, u32[]{:S(2)}) collective-permute-start(bf16[2,128,4,128]{1,3,2,0:T(8,128)(2,1)S(1)} %pad_maximum_fusion), channel_id=1, source_target_pairs={{0,4},{4,8},{8,12},{1,5},{5,9},{9,13},{2,6},{6,10},{10,14},{3,7},{... | collective-permute-start | bytes 786440 | tf_op jit(solution)/shard_map/ppermute | solution.py:20
  62.3 5.3 %collective-permute-start.1 = (bf16[2,128,4,128]{1,3,2,0:T(8,128)(2,1)S(1)}, bf16[2,128,4,128]{1,3,2,0:T(8,128)(2,1)S(1)}, u32[]{:S(2)}, u32[]{:S(2)}) collective-permute-start(bf16[2,128,4,128]{1,3,2,0:T(8,128)(2,1)S(1)} %collective-permute-done), channel_id=1, source_target_pairs={{0,4},{4,8},{8,12},{1,5},{5,9},{9,13},{2,6},{6,10},{10,14},{3,7},{... | collective-permute-start | bytes 786440 | tf_op jit(solution)/shard_map/ppermute | solution.py:20
  67.6 5.2 %collective-permute-start.2 = (bf16[2,128,4,128]{1,3,2,0:T(8,128)(2,1)S(1)}, bf16[2,128,4,128]{1,3,2,0:T(8,128)(2,1)S(1)}, u32[]{:S(2)}, u32[]{:S(2)}) collective-permute-start(bf16[2,128,4,128]{1,3,2,0:T(8,128)(2,1)S(1)} %collective-permute-done.1), channel_id=1, source_target_pairs={{0,4},{4,8},{8,12},{1,5},{5,9},{9,13},{2,6},{6,10},{10,14},{3,7},{... | collective-permute-start | bytes 786440 | tf_op jit(solution)/shard_map/ppermute | solution.py:20
  151.3 2.2 %copy-start.2 = (bf16[128,5376]{0,1:T(8,128)(2,1)S(1)}, bf16[128,5376]{0,1:T(8,128)(2,1)}, u32[]{:S(2)}) copy-start(bf16[128,5376]{0,1:T(8,128)(2,1)} %all-reduce.2.cloned.1.call-done) | copy-start | bytes 4128772
  153.5 1.0 copy-start.3
Sparse Core Ops, SparseCore 0:
  8.9 36.3 all-gather.1
  84.3 66.9 all-reduce.1
where the time goes:
time: 163 us; the launch traced here: 162 us
  waiting for transfers between devices  80.2 us (49%)
  local copies, waits for them, and re-layouts  27.8 us (17%)
  matrix products  23.8 us (15%)
  between operations  13.7 us (8%)
  starting transfers between devices  9.72 us (6%)
  other arithmetic  7.11 us (4%)
    psum x1, waiting for transfers between devices, per_device(): lax.psum(partial_value.astype(jnp.bfloat16), 'tp').astype(jnp.float32)  66.4 us
    dot_general x2, local copies, waits for them, and re-layouts, per_device(): key_raw = jnp.dot(normed, kv_full[0], preferred_element_type=jnp.float32)  17.3 us
    all_gather x1, waiting for transfers between devices, per_device(): lax.all_gather(tokens, 'tp', axis=1, tiled=True).astype(jnp.float32)  11.8 us
    ppermute x3, starting transfers between devices, passed_along(): return lax.ppermute(block, axis, route)  9.68 us
    dot_general x1, matrix products, per_device(): jnp.dot(attn, out_weight, preferred_element_type=jnp.float32)  9.61 us
    dot_general x1, local copies, waits for them, and re-layouts, per_device(): value_raw = jnp.dot(normed, kv_full[1], preferred_element_type=jnp.float32)  8.26 us
    dot_general x1, matrix products, per_device(): jnp.dot(normed, query_weight, preferred_element_type=jnp.float32)  6.44 us
    dot_general x1, matrix products, per_device(): key_raw = jnp.dot(normed, kv_full[0], preferred_element_type=jnp.float32)  4.84 us
  transfers between devices with their start and end apart: 5, of which 4 were waited for; matrix products, arithmetic and copies ran while one was open for 21% of the time, Pallas kernels for 0%

commit v1 on v0

--- a/solution.py
+++ b/solution.py
@@ -74,7 +74,9 @@
             jnp.concatenate([kv_weight, partner], axis=2),
             jnp.concatenate([partner, kv_weight], axis=2),
         )
-    gathered = lax.all_gather(tokens, "tp", axis=1, tiled=True).astype(jnp.float32)
+    gathered = jnp.concatenate(
+        lax.all_to_all(jnp.stack([tokens] * lax.axis_size("tp")), "tp", 0, 0), axis=1
+    ).astype(jnp.float32)
     normed = rms_norm(gathered, input_gain).astype(jnp.bfloat16)
     query_raw = jnp.dot(normed, query_weight, preferred_element_type=jnp.float32)
     key_raw = jnp.dot(normed, kv_full[0], preferred_element_type=jnp.float32)

time: 163 us -> 173 us (1.061)
  local copies, waits for them, and re-layouts: 27.8 us -> 43.9 us
  waiting for transfers between devices: 80.2 us -> 71.7 us
  starting transfers between devices: 9.72 us -> 13.9 us
    dot_general x0 -> x1, local copies, waits for them, and re-layouts: none -> 14.5 us  [per_device(): jnp.dot(normed, query_weight, preferred_element_type=jnp.float32)]
    all_gather x1 -> x0, waiting for transfers between devices: 11.8 us -> none  [per_device(): lax.all_gather(tokens, 'tp', axis=1, tiled=True).astype(jnp.float32)]
    all_to_all x0 -> x1, waiting for transfers between devices: none -> 7.34 us  [per_device(): lax.all_to_all(jnp.stack([tokens] * lax.axis_size('tp')), 'tp', 0, 0)]
    all_to_all x0 -> x1, starting transfers between devices: none -> 6.35 us  [per_device(): lax.all_to_all(jnp.stack([tokens] * lax.axis_size('tp')), 'tp', 0, 0)]
    psum x1, waiting for transfers between devices: 66.4 us -> 64 us  [per_device(): lax.psum(partial_value.astype(jnp.bfloat16), 'tp').astype(jnp.float32)]
    another operation x0 -> x1, local copies, waits for them, and re-layouts: none -> 2.24 us  [per_device(): jnp.stack([tokens] * lax.axis_size('tp'))]
    ppermute x3, starting transfers between devices: 9.68 us -> 7.53 us  [passed_along(): return lax.ppermute(block, axis, route)]
    reduce_sum x3 -> x2, other arithmetic: 4.44 us -> 2.89 us  [rms_norm(): jnp.mean(values * values, axis=-1, keepdims=True) + EPSILON]
  transfers between devices with their start and end apart: 5 -> 5, of which waited for: 4 -> 3; matrix products, arithmetic and copies ran while one was open for 21% -> 27% of each run, Pallas kernels for 0% -> 0%
where the time goes in v1:
time: 173 us; the launch traced here: 172 us
  waiting for transfers between devices  71.7 us (41%)
  local copies, waits for them, and re-layouts  43.9 us (25%)
  matrix products  22.6 us (13%)
  starting transfers between devices  13.9 us (8%)
  between operations  13.6 us (8%)
  other arithmetic  6.16 us (4%)
    psum x1, waiting for transfers between devices, per_device(): lax.psum(partial_value.astype(jnp.bfloat16), 'tp').astype(jnp.float32)  64 us
    dot_general x2, local copies, waits for them, and re-layouts, per_device(): key_raw = jnp.dot(normed, kv_full[0], preferred_element_type=jnp.float32)  17.2 us
    dot_general x1, local copies, waits for them, and re-layouts, per_device(): jnp.dot(normed, query_weight, preferred_element_type=jnp.float32)  14.5 us
    dot_general x1, matrix products, per_device(): jnp.dot(attn, out_weight, preferred_element_type=jnp.float32)  9.61 us
    dot_general x1, local copies, waits for them, and re-layouts, per_device(): value_raw = jnp.dot(normed, kv_full[1], preferred_element_type=jnp.float32)  7.92 us
    ppermute x3, starting transfers between devices, passed_along(): return lax.ppermute(block, axis, route)  7.53 us
    all_to_all x1, waiting for transfers between devices, per_device(): lax.all_to_all(jnp.stack([tokens] * lax.axis_size('tp')), 'tp', 0, 0)  7.34 us
    all_to_all x1, starting transfers between devices, per_device(): lax.all_to_all(jnp.stack([tokens] * lax.axis_size('tp')), 'tp', 0, 0)  6.35 us
  transfers between devices with their start and end apart: 5, of which 3 were waited for; matrix products, arithmetic and copies ran while one was open for 27% of the time, Pallas kernels for 0%

profile of v1, /device:TPU:0, one launch (start us, length us, event | category | flops | bytes accessed | tf_op | source)
XLA Modules:
  0.0 171.8 jit_solution(9062679834523414320)
XLA Ops:
  6.5 2.2 %stack.6 = bf16[4,128,1344]{1,2,0:T(8,128)(2,1)} broadcast(bf16[128,1344]{0,1:T(8,128)(2,1)} %param.10), dimensions={1,2} | broadcast | bytes 1720320 | tf_op jit(solution)/shard_map/stack | solution.py:78
  8.8 6.3 %all-to-all-start = ((bf16[4,128,1344]{1,2,0:T(8,128)(2,1)}), bf16[4,128,1344]{1,2,0:T(8,128)(2,1)S(1)}, u32[]{:S(2)}, u32[]{:S(2)}) async-start(bf16[4,128,1344]{1,2,0:T(8,128)(2,1)} %stack.6), calls=%async_computation | async-start | bytes 2752512 | tf_op jit(solution)/shard_map/all_to_all | solution.py:78
  15.2 9.0 %slice_bitcast_fusion.1 = (bf16[512,5376]{0,1:T(8,128)(2,1)}, bf16[512,5376]{0,1:T(8,128)(2,1)}) fusion(bf16[2,5376,512]{2,1,0:T(8,128)(2,1)} %param.15), kind=kLoop, calls=%fused_computation.2 | loop fusion | bytes 22020096 | tf_op jit(solution)/shard_map/dot_general | solution.py:82
  24.2 8.2 %copy.35 = bf16[512,5376]{1,0:T(8,128)(2,1)} copy(bf16[512,5376]{0,1:T(8,128)(2,1)} %get-tuple-element.5) | data formatting | bytes 11010048 | tf_op jit(solution)/shard_map/dot_general | solution.py:82
  32.4 7.9 %copy.37 = bf16[512,5376]{1,0:T(8,128)(2,1)} copy(bf16[512,5376]{0,1:T(8,128)(2,1)} %get-tuple-element.6) | data formatting | bytes 11010048 | tf_op jit(solution)/shard_map/dot_general | solution.py:83
  40.3 0.2 multiply_cosine_fusion
  40.5 7.3 %all-to-all-done = bf16[4,128,1344]{1,2,0:T(8,128)(2,1)S(1)} async-done(((bf16[4,128,1344]{1,2,0:T(8,128)(2,1)}), bf16[4,128,1344]{1,2,0:T(8,128)(2,1)S(1)}, u32[]{:S(2)}, u32[]{:S(2)}) %all-to-all-start) | async-done | bytes 1376288 | tf_op jit(solution)/shard_map/all_to_all | solution.py:78
  47.9 0.7 fusion
  48.6 0.9 fusion.2
  49.5 4.3 %multiply_reduce_fusion.2 = (f32[128,4]{0,1:T(4,128)S(1)}, f32[128,4,128]{0,2,1:T(8,128)S(1)}) fusion(bf16[128,5376,1]{0,1,2:T(8,128)(2,1)S(1)} %bitcast.72, bf16[4,128,5376]{2,1,0:T(8,128)(2,1)} %bitcast.70), kind=kOutput, calls=%fused_computation.39 | convolution fusion | flops 704773632 | bytes 7145472 | tf_op jit(solution)/shard_map/dot_general | solution.py:82
  53.9 1.6 fusion.8
  55.6 1.3 collective-permute-start
  57.0 14.5 %copy.60 = bf16[1024,5376]{1,0:T(8,128)(2,1)} copy(bf16[1024,5376]{0,1:T(8,128)(2,1)} %bitcast.75) | data formatting | bytes 22020096 | tf_op jit(solution)/shard_map/dot_general | solution.py:81
  71.4 0.1 compare_and_fusion
  71.6 4.1 %collective-permute-start.1 = (bf16[2,128,4,128]{1,3,2,0:T(8,128)(2,1)S(1)}, bf16[2,128,4,128]{1,3,2,0:T(8,128)(2,1)S(1)}, u32[]{:S(2)}, u32[]{:S(2)}) collective-permute-start(bf16[2,128,4,128]{1,3,2,0:T(8,128)(2,1)S(1)} %collective-permute-done), channel_id=1, source_target_pairs={{0,4},{4,8},{8,12},{1,5},{5,9},{9,13},{2,6},{6,10},{10,14},{3,7},{... | collective-permute-start | bytes 786440 | tf_op jit(solution)/shard_map/ppermute | solution.py:20
  75.7 5.8 %multiply_reduce_fusion.1 = (f32[128,8]{0,1:T(8,128)S(1)}, f32[128,8,128]{0,2,1:T(8,128)S(1)}) fusion(bf16[128,5376,1]{0,1,2:T(8,128)(2,1)S(1)} %bitcast.74, bf16[8,128,5376]{2,1,0:T(8,128)(2,1)} %bitcast.69), kind=kOutput, calls=%fused_computation.33 | convolution fusion | flops 1409547264 | bytes 12914688 | tf_op jit(solution)/shard_map/dot_general | solution.py:81
  81.6 2.1 %collective-permute-start.2 = (bf16[2,128,4,128]{1,3,2,0:T(8,128)(2,1)S(1)}, bf16[2,128,4,128]{1,3,2,0:T(8,128)(2,1)S(1)}, u32[]{:S(2)}, u32[]{:S(2)}) collective-permute-start(bf16[2,128,4,128]{1,3,2,0:T(8,128)(2,1)S(1)} %collective-permute-done.1), channel_id=1, source_target_pairs={{0,4},{4,8},{8,12},{1,5},{5,9},{9,13},{2,6},{6,10},{10,14},{3,7},{... | collective-permute-start | bytes 786440 | tf_op jit(solution)/shard_map/ppermute | solution.py:20
  83.7 0.1 multiply_multiply_fusion
  83.9 0.2 copy.42
  84.1 0.2 copy.43
  84.3 0.3 collective-permute-done.2
  84.7 0.1 maximum_maximum_fusion
  84.8 0.6 fusion.3
  85.4 0.4 fusion.4
  85.8 0.6 fusion.7
  86.4 9.6 %convolution_convert_fusion = bf16[128,5376]{0,1:T(8,128)(2,1)} fusion(bf16[128,1024]{0,1:T(8,128)(2,1)S(1)} %bitcast.78, bf16[1024,5376]{1,0:T(8,128)(2,1)} %param.18), kind=kOutput, calls=%fused_computation | convolution fusion | flops 1409974272 | bytes 12648448 | tf_op jit(solution)/shard_map/dot_general | solution.py:123
  96.0 0.8 dynamic-slice
  96.8 64.0 %all-reduce.2.cloned.1.call-done = bf16[128,5376]{0,1:T(8,128)(2,1)} async-done(((bf16[128,5376]{0,1:T(8,128)(2,1)}), bf16[128,5376]{0,1:T(8,128)(2,1)}) %all-reduce.2.cloned.1.call-update) | async-done | bytes 1376272 | tf_op jit(solution)/shard_map/psum | solution.py:124
  160.8 2.2 %multiply_reduce_fusion = f32[128]{0:T(128)S(1)} fusion(bf16[128,5376]{0,1:T(8,128)(2,1)} %all-reduce.2.cloned.1.call-done), kind=kLoop, calls=%fused_computation.8 | loop fusion | flops 2064256 | bytes 1376768 | tf_op jit(solution)/shard_map/reduce_sum | solution.py:25
  163.0 0.2 convert_element_type.67
  163.2 0.8 copy-done.2
  163.9 1.0 fusion.15
  (32 shorter events, 0.4 us)
Async XLA Ops:
  6.5 8.6 %copy-start.3 = (f32[5376]{0:T(1024)S(1)}, f32[5376]{0:T(1024)}, u32[]{:S(2)}) copy-start(f32[5376]{0:T(1024)} %param.13) | copy-start | bytes 64516
  8.8 39.1 %all-to-all-start = ((bf16[4,128,1344]{1,2,0:T(8,128)(2,1)}), bf16[4,128,1344]{1,2,0:T(8,128)(2,1)S(1)}, u32[]{:S(2)}, u32[]{:S(2)}) async-start(bf16[4,128,1344]{1,2,0:T(8,128)(2,1)} %stack.6), calls=%async_computation | async-start | bytes 2752512 | tf_op jit(solution)/shard_map/all_to_all | solution.py:78
  15.1 145.7 %all-reduce.2.cloned.1.call-start = ((), (), s32[]{:S(2)}) async-start(), calls=%async_computation.1 | async-start | bytes 2752512 | tf_op jit(solution)/shard_map/psum | solution.py:124
  24.2 8.2 %copy-start.7 = (s32[128]{0:T(128)S(1)}, s32[128]{0:T(128)}, u32[]{:S(2)}) copy-start(s32[128]{0:T(128)} %param.11) | copy-start | bytes 1540
  49.5 4.3 %copy-start = (bf16[512,5376]{1,0:T(8,128)(2,1)S(1)}, bf16[512,5376]{1,0:T(8,128)(2,1)}, u32[]{:S(2)}) copy-start(bf16[512,5376]{1,0:T(8,128)(2,1)} %copy.37) | copy-start | bytes 16515076
  53.9 1.6 copy-start.4
  55.6 16.0 %collective-permute-start = (bf16[2,128,4,128]{1,3,2,0:T(8,128)(2,1)S(1)}, bf16[2,128,4,128]{1,3,2,0:T(8,128)(2,1)S(1)}, u32[]{:S(2)}, u32[]{:S(2)}) collective-permute-start(bf16[2,128,4,128]{1,3,2,0:T(8,128)(2,1)S(1)} %pad_maximum_fusion), channel_id=1, source_target_pairs={{0,4},{4,8},{8,12},{1,5},{5,9},{9,13},{2,6},{6,10},{10,14},{3,7},{... | collective-permute-start | bytes 786440 | tf_op jit(solution)/shard_map/ppermute | solution.py:20
  57.0 14.5 %copy-start.5 = (s32[128]{0:T(128)S(1)}, s32[128]{0:T(128)}, u32[]{:S(2)}) copy-start(s32[128]{0:T(128)} %param.12) | copy-start | bytes 1540
  71.6 10.0 %collective-permute-start.1 = (bf16[2,128,4,128]{1,3,2,0:T(8,128)(2,1)S(1)}, bf16[2,128,4,128]{1,3,2,0:T(8,128)(2,1)S(1)}, u32[]{:S(2)}, u32[]{:S(2)}) collective-permute-start(bf16[2,128,4,128]{1,3,2,0:T(8,128)(2,1)S(1)} %collective-permute-done), channel_id=1, source_target_pairs={{0,4},{4,8},{8,12},{1,5},{5,9},{9,13},{2,6},{6,10},{10,14},{3,7},{... | collective-permute-start | bytes 786440 | tf_op jit(solution)/shard_map/ppermute | solution.py:20
  75.7 8.0 %copy-start.6 = (f32[128]{0:T(128)S(1)}, f32[128]{0:T(128)}, u32[]{:S(2)}) copy-start(f32[128]{0:T(128)} %param.16) | copy-start | bytes 1540
  81.6 3.0 %collective-permute-start.2 = (bf16[2,128,4,128]{1,3,2,0:T(8,128)(2,1)S(1)}, bf16[2,128,4,128]{1,3,2,0:T(8,128)(2,1)S(1)}, u32[]{:S(2)}, u32[]{:S(2)}) collective-permute-start(bf16[2,128,4,128]{1,3,2,0:T(8,128)(2,1)S(1)} %collective-permute-done.1), channel_id=1, source_target_pairs={{0,4},{4,8},{8,12},{1,5},{5,9},{9,13},{2,6},{6,10},{10,14},{3,7},{... | collective-permute-start | bytes 786440 | tf_op jit(solution)/shard_map/ppermute | solution.py:20
  160.8 2.2 %copy-start.1 = (bf16[128,5376]{0,1:T(8,128)(2,1)S(1)}, bf16[128,5376]{0,1:T(8,128)(2,1)}, u32[]{:S(2)}) copy-start(bf16[128,5376]{0,1:T(8,128)(2,1)} %all-reduce.2.cloned.1.call-done) | copy-start | bytes 4128772
  163.0 1.0 copy-start.2
Sparse Core Ops, SparseCore 0:
  96.2 64.5 all-reduce.1
